TPU v7x, 32 devices: a whole 2x2x4 slice. The times are simulated.
32 devices in a mesh: grp: 2 (over y), src: 8 (over z, x), tgt: 2 (over core).
Axes of the slice: x: 2, y: 2, z: 4, core: 2. Of those that a mesh axis runs over, the one named last changes fastest.
Arguments:
- source_feat: float32 [256, 64, 128], P(('grp', 'src')), parts along dimension 0, may hold values from -1.2 to 1.2
- target_feat: float32 [32, 64, 128], P(('grp', 'src', 'tgt')), parts along dimension 0, may hold values from -1.2 to 1.2
- log_mass_src: float32 [256, 128], P(('grp', 'src')), parts along dimension 0, may hold values from -3 to 3
- log_mass_tgt: float32 [32, 128], P(('grp', 'src', 'tgt')), parts along dimension 0, may hold values from -3 to 3
- potential_tgt: float32 [32, 128], P(('grp', 'src', 'tgt')), parts along dimension 0, may hold values from -6 to 152
- support: int32 [256, 2, 8], P(('grp', 'src'), 'tgt'), parts along dimension 0, may hold values from 0 to 7, as said below
- counts: int32 [256, 2], P(('grp', 'src'), 'tgt'), parts along dimension 0, may hold values from 1 to 8, as said below
Outputs:
- potential_src: float32 [256, 128], P(('grp', 'src')), parts along dimension 0
- potential_new: float32 [32, 128], P(('grp', 'src', 'tgt')), parts along dimension 0
There are 2 independent parts, one for each index of `grp`. A program takes and returns all parts, laid end to end along the dimension named above; each array names one. Nothing has to cross between parts.
Inputs may be any that keep to these rules, and one draw needn't show every extreme that they name: `support`: within one list the first counts entries are distinct; unused entries are also valid indices and are ignored; every target block of a shard is named within the used entries of some source block row. `counts`: the source block rows of one index of src share a load level, so some devices use far more slots than others; some list is full in every draw.
All inputs are finite; a program needn't handle non-finite values.
Results may differ from a plain program's by a relative error of at most 0.000096.
Values sent between devices are 32-bit elements; how exact they have to be, the bound alone decides.
A program may use at most 64 MiB of HBM per device.

v0:
```python
import math

import jax
import jax.numpy as jnp
from jax import lax
from jax.sharding import PartitionSpec as P

entropic = 0.5
very_low = -1e30


def merged(part, axis, combine):
    gathered = jax.tree.map(lambda a: lax.all_gather(a, axis), part)

    def take(source):
        return jax.tree.map(lambda a: lax.dynamic_index_in_dim(a, source, 0, False), gathered)

    return lax.fori_loop(
        1, lax.axis_size(axis), lambda source, state: combine(state, take(source)), take(0)
    )


def cost_tiles(source_blk, source_sq, target_blk, target_sq):
    cross = jnp.einsum(
        "...fi,...fj->...ij", source_blk, target_blk, precision=lax.Precision.HIGHEST
    )
    return source_sq[..., :, None] + target_sq[..., None, :] - 2.0 * cross


def row_stats(cost, mass_tgt, poten_tgt, usable):
    scores = mass_tgt[..., None, :] + (poten_tgt[..., None, :] - cost) / entropic
    scores = jnp.where(usable[..., None, None], scores, very_low)
    peak = jnp.max(scores, axis=(1, 3))
    total = jnp.sum(jnp.exp(scores - peak[:, None, :, None]), axis=(1, 3))
    return (peak, total)


def column_stats(cost, mass_src, poten_src, usable):
    scores = mass_src[:, None, :, None] + (poten_src[:, None, :, None] - cost) / entropic
    peak = jnp.max(scores, axis=2)
    total = jnp.sum(jnp.exp(scores - peak[:, :, None, :]), axis=2)
    peak = jnp.where(usable[..., None], peak, very_low)
    total = jnp.where(usable[..., None], total, 0.0)
    return (peak, total)


def merge_pair(first_pair, second_pair):
    first_peak, first_total = first_pair
    second_peak, second_total = second_pair
    highest = jnp.maximum(first_peak, second_peak)
    summed = first_total * jnp.exp(first_peak - highest) + second_total * jnp.exp(
        second_peak - highest
    )
    return (highest, summed)


def segment_merge(peaks, totals, seg_ids, segments):
    best = jax.ops.segment_max(peaks, seg_ids, num_segments=segments + 1)
    best = jnp.maximum(best, very_low)
    summed = jax.ops.segment_sum(
        totals * jnp.exp(peaks - best[seg_ids]), seg_ids, num_segments=segments + 1
    )
    return (best[:segments], summed[:segments])


def per_device(
    source_feat, target_feat, log_mass_src, log_mass_tgt, potential_tgt, support, counts
):
    target_all, mass_all, poten_all = (
        lax.all_gather(target_feat, "src", axis=0, tiled=True),
        lax.all_gather(log_mass_tgt, "src", axis=0, tiled=True),
        lax.all_gather(potential_tgt, "src", axis=0, tiled=True),
    )
    blocks = target_all.shape[0]
    rows_here = source_feat.shape[0]
    slots_here = support.shape[2]
    cells = source_feat.shape[2]
    indices = support[:, 0, :]
    limits = counts[:, 0]
    usable = jnp.arange(slots_here, dtype=jnp.int32)[None, :] < limits[:, None]
    source_sq = jnp.sum(source_feat * source_feat, axis=1)
    target_sq = jnp.sum(target_all * target_all, axis=1)
    width = math.gcd(rows_here, 4)

    def grouped(array):
        return array.reshape((rows_here // width, width) + array.shape[1:])

    def row_pass(items):
        source_blk, source_nrm, ids_here, use_here = items
        cost = cost_tiles(
            source_blk[:, None], source_nrm[:, None], target_all[ids_here], target_sq[ids_here]
        )
        return row_stats(cost, mass_all[ids_here], poten_all[ids_here], use_here)

    peak, total = lax.map(
        row_pass, (grouped(source_feat), grouped(source_sq), grouped(indices), grouped(usable))
    )
    peak = peak.reshape(rows_here, cells)
    total = total.reshape(rows_here, cells)
    peak_all, total_all = merged((peak, total), "tgt", merge_pair)
    potential_src = -entropic * (peak_all + jnp.log(total_all))

    def column_pass(items):
        source_blk, source_nrm, mass_here, poten_here, ids_here, use_here = items
        cost = cost_tiles(
            source_blk[:, None], source_nrm[:, None], target_all[ids_here], target_sq[ids_here]
        )
        return column_stats(cost, mass_here, poten_here, use_here)

    peaks, totals = lax.map(
        column_pass,
        (
            grouped(source_feat),
            grouped(source_sq),
            grouped(log_mass_src),
            grouped(potential_src),
            grouped(indices),
            grouped(usable),
        ),
    )
    seg_ids = jnp.where(usable, indices, blocks).reshape(-1)
    best, summed = segment_merge(
        peaks.reshape(-1, cells), totals.reshape(-1, cells), seg_ids, blocks
    )
    share = blocks // lax.axis_size("src")
    own_start = lax.axis_index("src") * share
    highest = lax.pmax(best, "src")
    whole = lax.psum(summed * jnp.exp(best - highest), "src")
    own_peak = lax.dynamic_slice_in_dim(highest, own_start, share, 0)
    own_total = lax.dynamic_slice_in_dim(whole, own_start, share, 0)
    potential_new = -entropic * (own_peak + jnp.log(own_total))
    return (potential_src, potential_new)


def solution(mesh):
    in_specs = (
        P(("grp", "src"), None, None),
        P(("grp", "src", "tgt"), None, None),
        P(("grp", "src"), None),
        P(("grp", "src", "tgt"), None),
        P(("grp", "src", "tgt"), None),
        P(("grp", "src"), "tgt", None),
        P(("grp", "src"), "tgt"),
    )
    out_specs = (P(("grp", "src"), None), P(("grp", "src", "tgt"), None))
    return jax.shard_map(
        per_device, mesh=mesh, in_specs=in_specs, out_specs=out_specs, check_vma=False
    )
```

profile of v0, /device:TPU:0, one launch (start us, length us, event | category | flops | bytes accessed | tf_op | source)
XLA Modules:
  0.0 177.2 jit_solution(18147925197401593971)
XLA Ops:
  1.2 1.3 reduce.3
  2.6 0.8 copy.19
  3.4 22.4 %all-gather = f32[8,1,128]{2,1,0:T(1,128)S(1)} all-gather(f32[1,1,128]{2,1,0:T(1,128)} %bitcast.189), channel_id=1, replica_groups=mesh['grp'=2,'src'=8,'tgt'=2] {'src'}, dimensions={0}, use_global_device_ids=true | all-gather | bytes 4608 | tf_op jit(solution)/shard_map/all_gather | solution.py:71
  25.8 16.5 %all-gather.1 = f32[8,1,128]{2,1,0:T(1,128)S(1)} all-gather(f32[1,1,128]{2,1,0:T(1,128)} %bitcast.190), channel_id=1, replica_groups=mesh['grp'=2,'src'=8,'tgt'=2] {'src'}, dimensions={0}, use_global_device_ids=true | all-gather | bytes 4608 | tf_op jit(solution)/shard_map/all_gather | solution.py:72
  42.3 1.1 multiply_reduce_fusion
  43.4 31.0 %all_gather.17 = f32[8,64,128]{2,1,0:T(8,128)S(1)} all-gather(f32[1,64,128]{2,1,0:T(8,128)} %param.12), channel_id=1, replica_groups=mesh['grp'=2,'src'=8,'tgt'=2] {'src'}, dimensions={0}, use_global_device_ids=true | all-gather | bytes 294912 | tf_op jit(solution)/shard_map/all_gather | solution.py:70
  74.5 35.7 %while.8 = (s32[]{:T(128)}, f32[4,4,128]{2,1,0:T(4,128)S(1)}, f32[4,4,128]{2,1,0:T(4,128)S(1)}, pred[4,4,8]{2,1,0:T(4,128)(4,1)S(1)}, s32[4,4,8]{2,1,0:T(4,128)S...) while((s32[]{:T(128)}, f32[4,4,128]{2,1,0:T(4,128)S(1)}, ...), condition=%wide.region_5.6_spmd, body=%wide.region_2.5_spmd.sunk | while | flops 407896160 | bytes 7644529 | solution.py:95
  77.0 6.1 %fusion.44 = (f32[4,128]{1,0:T(4,128)S(1)}, f32[4,8,128,128]{2,3,1,0:T(8,128)S(1)}) fusion(f32[4,8,64,128]{3,2,1,0:T(8,128)S(1)} %bitcast.172, f32[4,4,64,128]{3,2,1,0:T(8,128)} %get-tuple-element.388, s32[]{:T(128)S(6)} %copy.30, f32[4,8,128]{2,1,0:T(8,128)S(1)} %bitcast.175, f32[4,128]{1,0:T(4,128)S(1)} %dynamic-slice_bitcast_fusion.9, ...), kind=kOutput, calls=%fused_computation.75.clone.1 | convolution fusion | flops 406846976 | bytes 3330084 | tf_op jit(solution)/shard_map/while/body/eval_jaxpr/...fi,...fj->...ij/dot_general | solution.py:24
  85.9 6.1 %fusion.44 = (f32[4,128]{1,0:T(4,128)S(1)}, f32[4,8,128,128]{2,3,1,0:T(8,128)S(1)}) fusion(f32[4,8,64,128]{3,2,1,0:T(8,128)S(1)} %bitcast.172, f32[4,4,64,128]{3,2,1,0:T(8,128)} %get-tuple-element.388, s32[]{:T(128)S(6)} %copy.30, f32[4,8,128]{2,1,0:T(8,128)S(1)} %bitcast.175, f32[4,128]{1,0:T(4,128)S(1)} %dynamic-slice_bitcast_fusion.9, ...), kind=kOutput, calls=%fused_computation.75.clone.1 | convolution fusion | flops 406846976 | bytes 3330084 | tf_op jit(solution)/shard_map/while/body/eval_jaxpr/...fi,...fj->...ij/dot_general | solution.py:24
  94.8 6.1 %fusion.44 = (f32[4,128]{1,0:T(4,128)S(1)}, f32[4,8,128,128]{2,3,1,0:T(8,128)S(1)}) fusion(f32[4,8,64,128]{3,2,1,0:T(8,128)S(1)} %bitcast.172, f32[4,4,64,128]{3,2,1,0:T(8,128)} %get-tuple-element.388, s32[]{:T(128)S(6)} %copy.30, f32[4,8,128]{2,1,0:T(8,128)S(1)} %bitcast.175, f32[4,128]{1,0:T(4,128)S(1)} %dynamic-slice_bitcast_fusion.9, ...), kind=kOutput, calls=%fused_computation.75.clone.1 | convolution fusion | flops 406846976 | bytes 3330084 | tf_op jit(solution)/shard_map/while/body/eval_jaxpr/...fi,...fj->...ij/dot_general | solution.py:24
  103.8 6.1 %fusion.44 = (f32[4,128]{1,0:T(4,128)S(1)}, f32[4,8,128,128]{2,3,1,0:T(8,128)S(1)}) fusion(f32[4,8,64,128]{3,2,1,0:T(8,128)S(1)} %bitcast.172, f32[4,4,64,128]{3,2,1,0:T(8,128)} %get-tuple-element.388, s32[]{:T(128)S(6)} %copy.30, f32[4,8,128]{2,1,0:T(8,128)S(1)} %bitcast.175, f32[4,128]{1,0:T(4,128)S(1)} %dynamic-slice_bitcast_fusion.9, ...), kind=kOutput, calls=%fused_computation.75.clone.1 | convolution fusion | flops 406846976 | bytes 3330084 | tf_op jit(solution)/shard_map/while/body/eval_jaxpr/...fi,...fj->...ij/dot_general | solution.py:24
  110.2 1.8 %all_gather.19 = f32[2,16,128]{2,1,0:T(8,128)S(1)} all-gather(f32[1,16,128]{2,1,0:T(8,128)S(1)} %bitcast.188), channel_id=1, replica_groups=mesh['grp'=2,'src'=8,'tgt'=2] {'tgt'}, dimensions={0}, use_global_device_ids=true | all-gather | bytes 24576 | tf_op jit(solution)/shard_map/all_gather | solution.py:13
  112.0 1.8 %all_gather.18 = f32[2,16,128]{2,1,0:T(8,128)S(1)} all-gather(f32[1,16,128]{2,1,0:T(8,128)S(1)} %bitcast.187), channel_id=1, replica_groups=mesh['grp'=2,'src'=8,'tgt'=2] {'tgt'}, dimensions={0}, use_global_device_ids=true | all-gather | bytes 24576 | tf_op jit(solution)/shard_map/all_gather | solution.py:13
  114.8 22.8 %while.9 = (s32[]{:T(128)}, f32[4,4,8,128]{3,2,1,0:T(8,128)S(1)}, f32[4,4,8,128]{3,2,1,0:T(8,128)S(1)}, pred[4,4,8]{2,1,0:T(4,128)(4,1)S(1)}, f32[4,4,128]{2,1,0...) while((s32[]{:T(128)}, f32[4,4,8,128]{3,2,1,0:T(8,128)S(1)}, ...), condition=%wide.region_9.10_spmd, body=%wide.region_6.9_spmd.sunk | while | flops 407372896 | bytes 7659093 | solution.py:110
  116.2 0.7 dynamic-slice_bitcast_fusion.12
  116.9 3.2 %fusion.46 = (f32[4,8,128]{2,1,0:T(8,128)S(1)}, f32[4,8,128,128]{3,2,1,0:T(8,128)S(1)}) fusion(f32[4,8,64,128]{3,2,1,0:T(8,128)S(1)} %bitcast.171, f32[4,4,64,128]{3,2,1,0:T(8,128)} %get-tuple-element.424, s32[]{:T(128)S(6)} %copy.39, f32[4,8,128]{2,1,0:T(8,128)S(1)} %bitcast.174, f32[4,128]{1,0:T(4,128)S(1)} %get-tuple-element.348, ...), kind=kOutput, calls=%fused_computation.76.clone.1 | convolution fusion | flops 406319104 | bytes 3315716 | tf_op jit(solution)/shard_map/while/body/eval_jaxpr/...fi,...fj->...ij/dot_general | solution.py:24
  121.9 0.7 dynamic-slice_bitcast_fusion.12
  122.5 3.2 %fusion.46 = (f32[4,8,128]{2,1,0:T(8,128)S(1)}, f32[4,8,128,128]{3,2,1,0:T(8,128)S(1)}) fusion(f32[4,8,64,128]{3,2,1,0:T(8,128)S(1)} %bitcast.171, f32[4,4,64,128]{3,2,1,0:T(8,128)} %get-tuple-element.424, s32[]{:T(128)S(6)} %copy.39, f32[4,8,128]{2,1,0:T(8,128)S(1)} %bitcast.174, f32[4,128]{1,0:T(4,128)S(1)} %get-tuple-element.348, ...), kind=kOutput, calls=%fused_computation.76.clone.1 | convolution fusion | flops 406319104 | bytes 3315716 | tf_op jit(solution)/shard_map/while/body/eval_jaxpr/...fi,...fj->...ij/dot_general | solution.py:24
  128.2 3.2 %fusion.46 = (f32[4,8,128]{2,1,0:T(8,128)S(1)}, f32[4,8,128,128]{3,2,1,0:T(8,128)S(1)}) fusion(f32[4,8,64,128]{3,2,1,0:T(8,128)S(1)} %bitcast.171, f32[4,4,64,128]{3,2,1,0:T(8,128)} %get-tuple-element.424, s32[]{:T(128)S(6)} %copy.39, f32[4,8,128]{2,1,0:T(8,128)S(1)} %bitcast.174, f32[4,128]{1,0:T(4,128)S(1)} %get-tuple-element.348, ...), kind=kOutput, calls=%fused_computation.76.clone.1 | convolution fusion | flops 406319104 | bytes 3315716 | tf_op jit(solution)/shard_map/while/body/eval_jaxpr/...fi,...fj->...ij/dot_general | solution.py:24
  133.9 3.2 %fusion.46 = (f32[4,8,128]{2,1,0:T(8,128)S(1)}, f32[4,8,128,128]{3,2,1,0:T(8,128)S(1)}) fusion(f32[4,8,64,128]{3,2,1,0:T(8,128)S(1)} %bitcast.171, f32[4,4,64,128]{3,2,1,0:T(8,128)} %get-tuple-element.424, s32[]{:T(128)S(6)} %copy.39, f32[4,8,128]{2,1,0:T(8,128)S(1)} %bitcast.174, f32[4,128]{1,0:T(4,128)S(1)} %get-tuple-element.348, ...), kind=kOutput, calls=%fused_computation.76.clone.1 | convolution fusion | flops 406319104 | bytes 3315716 | tf_op jit(solution)/shard_map/while/body/eval_jaxpr/...fi,...fj->...ij/dot_general | solution.py:24
  137.6 1.0 scatter_custom_fusion
  139.4 1.0 scatter_custom_fusion.1
  140.4 19.1 %pmax.7 = f32[8,128]{1,0:T(8,128)S(1)} all-reduce(f32[8,128]{1,0:T(8,128)S(1)} %slice.26), channel_id=1, replica_groups=mesh['grp'=2,'src'=8,'tgt'=2] {'src'}, use_global_device_ids=true, to_apply=%region_11.12 | all-reduce | flops 1024 | bytes 8192 | tf_op jit(solution)/shard_map/pmax | solution.py:127
  159.6 17.1 %psum.7 = f32[8,128]{1,0:T(8,128)S(1)} all-reduce(f32[8,128]{1,0:T(8,128)S(1)} %slice_multiply_fusion), channel_id=1, replica_groups=mesh['grp'=2,'src'=8,'tgt'=2] {'src'}, use_global_device_ids=true, to_apply=%region_13.14 | all-reduce | flops 1024 | bytes 8192 | tf_op jit(solution)/shard_map/psum | solution.py:128
  (107 shorter events, 22.3 us)
Async XLA Ops:
  74.5 40.0 %copy-start = (s32[16,1]{0,1:T(1,128)S(1)}, s32[16,1]{0,1:T(1,128)}, u32[]{:S(2)}) copy-start(s32[16,1]{0,1:T(1,128)} %param.17) | copy-start | bytes 196
where the time goes:
time: 178 us; the launch traced here: 177 us
  blocking collectives  110 us (62%)
  matrix products  37.3 us (21%)
  local copies, waits for them, and re-layouts  19.9 us (11%)
  other arithmetic  8.98 us (5%)
    dot_general x8, matrix products, cost_tiles(): jnp.einsum('...fi,...fj->...ij', source_blk, target_blk, precision=lax.Pr...  37.3 us
    all_gather x1, blocking collectives, per_device(): lax.all_gather(target_feat, 'src', axis=0, tiled=True)  31 us
    all_gather x1, blocking collectives, per_device(): lax.all_gather(log_mass_tgt, 'src', axis=0, tiled=True)  22.4 us
    pmax x1, blocking collectives, per_device(): highest = lax.pmax(best, 'src')  19.1 us
    psum x1, blocking collectives, per_device(): whole = lax.psum(summed * jnp.exp(best - highest), 'src')  17.1 us
    all_gather x1, blocking collectives, per_device(): lax.all_gather(potential_tgt, 'src', axis=0, tiled=True)  16.5 us
    gather x8, local copies, waits for them, and re-layouts, row_pass(): return row_stats(cost, mass_all[ids_here], poten_all[ids_here], use_here)  4.59 us
    all_gather x2, blocking collectives, merged(): gathered = jax.tree.map(lambda a: lax.all_gather(a, axis), part)  3.63 us

commit v1 on v0

--- a/solution.py
+++ b/solution.py
@@ -1,8 +1,11 @@
+import functools
 import math
 
 import jax
 import jax.numpy as jnp
 from jax import lax
+from jax.experimental import pallas as pl
+from jax.experimental.pallas import tpu as pltpu
 from jax.sharding import PartitionSpec as P
 
 entropic = 0.5
@@ -63,7 +66,7 @@
     return (best[:segments], summed[:segments])
 
 
-def per_device(
+def general_path(
     source_feat, target_feat, log_mass_src, log_mass_tgt, potential_tgt, support, counts
 ):
     target_all, mass_all, poten_all = (
@@ -132,6 +135,309 @@
     return (potential_src, potential_new)
 
 
+LOG2E = 1.4426950408889634
+LN2 = 0.6931471805599453
+MESH = pl.DeviceIdType.MESH
+DENSE_BYTES = 24 * 1024 * 1024
+
+
+def split3(value):
+    high = value.astype(jnp.bfloat16).astype(jnp.float32)
+    rest = value - high
+    mid = rest.astype(jnp.bfloat16).astype(jnp.float32)
+    return high, mid, rest - mid
+
+
+def partner(me, step, count):
+    if count & (count - 1):
+        return (me + step) % count
+    met, bit = 0, 1
+    while bit < count:
+        met = met + bit * ((me // bit + step // bit) % 2)
+        bit *= 2
+    return met
+
+
+def origin(me, step, count):
+    if count & (count - 1):
+        return (me - step + count) % count
+    return partner(me, step, count)
+
+
+def sinkhorn_kernel(
+    n_src, n_tgt, chunk,
+    x_ref, y_ref, lms_ref, lmt_ref, pt_ref, sup_ref, cnt_ref,
+    ps_ref, pn_ref,
+    y_all, lm_all, pt_all, xt, scores, run_max, bias, peak_col, total_col, shift,
+    x_sq, stat_out, stat_in, col_out, col_in,
+    y_send, y_recv, s_send, s_recv, c_send, c_recv,
+):
+    rows, feats, cells = x_ref.shape
+    slots = sup_ref.shape[2]
+    grp = lax.axis_index("grp")
+    me = lax.axis_index("src")
+    shard = lax.axis_index("tgt")
+
+    barrier = pltpu.get_barrier_semaphore()
+    for step in range(1, n_src):
+        pl.semaphore_signal(
+            barrier, inc=1, device_id=(grp, partner(me, step, n_src), shard), device_id_type=MESH
+        )
+    for step in range(1, n_tgt):
+        pl.semaphore_signal(
+            barrier, inc=1, device_id=(grp, me, (shard + step) % n_tgt), device_id_type=MESH
+        )
+    pl.semaphore_wait(barrier, n_src - 1 + n_tgt - 1)
+
+    parts = ((y_ref, y_all), (lmt_ref, lm_all), (pt_ref, pt_all))
+
+    def target_copy(index, where, step, peer):
+        mine, everyone = parts[index]
+        return pltpu.make_async_remote_copy(
+            src_ref=mine,
+            dst_ref=everyone.at[pl.ds(where, 1)],
+            send_sem=y_send.at[index, step],
+            recv_sem=y_recv.at[index, where],
+            device_id=(grp, peer, shard),
+            device_id_type=MESH,
+        )
+
+    for step in range(1, n_src):
+        peer = partner(me, step, n_src)
+        for index in range(3):
+            target_copy(index, me, step, peer).start()
+    y_all[me] = y_ref[0]
+    lm_all[pl.ds(me, 1)] = lmt_ref[...]
+    pt_all[pl.ds(me, 1)] = pt_ref[...]
+
+    def prepare(row, carry):
+        x = x_ref[row]
+        x_sq[pl.ds(row, 1)] = jnp.sum(x * x, axis=0, keepdims=True)
+        high, mid, low = split3(x * (4.0 * LOG2E))
+        first = jnp.concatenate([high, mid], axis=0).T.astype(jnp.bfloat16)
+        second = jnp.concatenate([low, high], axis=0).T.astype(jnp.bfloat16)
+        here = pl.ds(row * cells, cells)
+        xt[here, 0 : 2 * feats] = first
+        xt[here, 2 * feats : 4 * feats] = first
+        xt[here, 4 * feats : 6 * feats] = second
+        return carry
+
+    lax.fori_loop(0, rows, prepare, 0)
+    run_max[...] = jnp.full(run_max.shape, 4.0 * very_low, jnp.float32)
+
+    limits = cnt_ref[...]
+    ids = sup_ref[:, 0, :]
+
+    def block_scores(block):
+        y = y_all[block]
+        high, mid, low = split3(y)
+        weights = jnp.concatenate([high, high, mid, mid, high, low], axis=0).astype(jnp.bfloat16)
+        y_sq = jnp.sum(y * y, axis=0, keepdims=True)
+        level = LOG2E * (
+            lm_all[pl.ds(block, 1)] + 2.0 * pt_all[pl.ds(block, 1)] - 2.0 * y_sq
+        )
+        joined = jnp.zeros((rows, 1), jnp.bool_)
+        for slot in range(slots):
+            joined = joined | ((ids[:, slot : slot + 1] == block) & (limits > slot))
+        bias[...] = level + jnp.where(joined, 0.0, very_low)
+        for start in range(0, rows, chunk):
+            here = slice(start * cells, (start + chunk) * cells)
+            cross = jnp.dot(xt[here, :], weights, preferred_element_type=jnp.float32)
+            for row in range(chunk):
+                tile = slice((start + row) * cells, (start + row + 1) * cells)
+                value = cross[row * cells : (row + 1) * cells] + bias[start + row : start + row + 1]
+                scores[block, tile] = value
+                run_max[tile] = jnp.maximum(run_max[tile], value)
+
+    block_scores(me)
+
+    def arrival(step, carry):
+        block = origin(me, step, n_src)
+        for index in range(3):
+            target_copy(index, block, step, block).wait_recv()
+        block_scores(block)
+        return carry
+
+    lax.fori_loop(1, n_src, arrival, 0)
+
+    lanes = lax.broadcasted_iota(jnp.int32, (cells, cells), 1)
+    peak_col[...] = jnp.zeros_like(peak_col)
+    total_col[...] = jnp.ones_like(total_col)
+
+    def row_block(row, carry):
+        here = pl.ds(row * cells, cells)
+        peak = jnp.max(run_max[here], axis=1, keepdims=True)
+        gathered = jnp.exp2(scores[0, here] - peak)
+        for block in range(1, n_src):
+            gathered = gathered + jnp.exp2(scores[block, here] - peak)
+        total = jnp.sum(gathered, axis=1, keepdims=True)
+        chosen = lanes == row
+        peak_col[...] = jnp.where(chosen, peak, peak_col[...])
+        total_col[...] = jnp.where(chosen, total, total_col[...])
+        return carry
+
+    lax.fori_loop(0, rows, row_block, 0)
+    own_peak = peak_col[...].T[:rows]
+    own_total = total_col[...].T[:rows]
+    stat_out[0] = own_peak
+    stat_out[1] = own_total
+
+    def stat_copy(where, step, peer):
+        return pltpu.make_async_remote_copy(
+            src_ref=stat_out,
+            dst_ref=stat_in.at[where],
+            send_sem=s_send.at[step],
+            recv_sem=s_recv.at[where],
+            device_id=(grp, me, peer),
+            device_id_type=MESH,
+        )
+
+    for step in range(1, n_tgt):
+        stat_copy(step, step, (shard + step) % n_tgt).start()
+    for step in range(1, n_src):
+        for index in range(3):
+            target_copy(index, me, step, partner(me, step, n_src)).wait_send()
+    for step in range(1, n_tgt):
+        stat_copy(step, step, (shard + step) % n_tgt).wait_recv()
+    peak, total = own_peak, own_total
+    for step in range(1, n_tgt):
+        other_peak, other_total = stat_in[step, 0], stat_in[step, 1]
+        highest = jnp.maximum(peak, other_peak)
+        total = total * jnp.exp2(peak - highest) + other_total * jnp.exp2(other_peak - highest)
+        peak = highest
+    joint = peak + jnp.log(total) * LOG2E
+    ps_ref[...] = x_sq[...] - (entropic * LN2) * joint
+    offset = LOG2E * lms_ref[...] - joint
+    offset = jnp.concatenate([offset, jnp.zeros((cells - rows, cells), jnp.float32)], axis=0).T
+    for row in range(rows):
+        shift[row * cells : (row + 1) * cells] = jnp.broadcast_to(
+            offset[:, row : row + 1], (cells, cells)
+        )
+
+    def column(block):
+        def highest(row, best):
+            here = pl.ds(row * cells, cells)
+            value = scores[block, here] + shift[here]
+            scores[block, here] = value
+            return jnp.maximum(best, jnp.max(value.reshape(cells // 8, 8, cells), axis=0))
+
+        best = lax.fori_loop(0, rows, highest, jnp.full((8, cells), 4.0 * very_low, jnp.float32))
+        best = jnp.max(best, axis=0, keepdims=True)
+
+        def add(row, summed):
+            here = pl.ds(row * cells, cells)
+            value = jnp.exp2(scores[block, here] - best)
+            return summed + jnp.sum(value.reshape(cells // 8, 8, cells), axis=0)
+
+        summed = lax.fori_loop(0, rows, add, jnp.zeros((8, cells), jnp.float32))
+        return best, jnp.sum(summed, axis=0, keepdims=True)
+
+    def column_copy(dest, where, step):
+        return pltpu.make_async_remote_copy(
+            src_ref=col_out.at[dest],
+            dst_ref=col_in.at[where],
+            send_sem=c_send.at[step],
+            recv_sem=c_recv.at[where],
+            device_id=(grp, dest, shard),
+            device_id_type=MESH,
+        )
+
+    def send_column(index, carry):
+        step = n_src - 1 - index
+        block = partner(me, step, n_src)
+        best, summed = column(block)
+        col_out[block, 0:1] = best
+        col_out[block, 1:2] = summed
+        column_copy(block, me, step).start()
+        return carry
+
+    lax.fori_loop(0, n_src - 1, send_column, 0)
+    best, summed = column(me)
+    col_in[me, 0:1] = best
+    col_in[me, 1:2] = summed
+    for step in range(1, n_src):
+        sender = origin(me, step, n_src)
+        column_copy(sender, sender, step).wait_recv()
+    peaks = col_in[:, 0, :]
+    totals = col_in[:, 1, :]
+    highest = jnp.max(peaks, axis=0, keepdims=True)
+    whole = jnp.sum(totals * jnp.exp2(peaks - highest), axis=0, keepdims=True)
+    pn_ref[...] = (
+        pt_ref[...]
+        + entropic * lmt_ref[...]
+        - (entropic * LN2) * (highest + jnp.log(whole) * LOG2E)
+    )
+    for step in range(1, n_tgt):
+        stat_copy(step, step, (shard + step) % n_tgt).wait_send()
+    for step in range(1, n_src):
+        column_copy(partner(me, step, n_src), me, step).wait_send()
+
+
+def dense_path(source_feat, target_feat, log_mass_src, log_mass_tgt, potential_tgt, support, counts):
+    n_src, n_tgt = lax.axis_size("src"), lax.axis_size("tgt")
+    rows, feats, cells = source_feat.shape
+    vmem = pl.BlockSpec(memory_space=pltpu.VMEM)
+    f32 = jnp.float32
+    dma = pltpu.SemaphoreType.DMA
+    return pl.pallas_call(
+        functools.partial(sinkhorn_kernel, n_src, n_tgt, math.gcd(rows, 4)),
+        out_shape=(
+            jax.ShapeDtypeStruct((rows, cells), f32),
+            jax.ShapeDtypeStruct((1, cells), f32),
+        ),
+        in_specs=[vmem] * 7,
+        out_specs=(vmem, vmem),
+        scratch_shapes=[
+            pltpu.VMEM((n_src, feats, cells), f32),
+            pltpu.VMEM((n_src, cells), f32),
+            pltpu.VMEM((n_src, cells), f32),
+            pltpu.VMEM((rows * cells, 6 * feats), jnp.bfloat16),
+            pltpu.VMEM((n_src, rows * cells, cells), f32),
+            pltpu.VMEM((rows * cells, cells), f32),
+            pltpu.VMEM((rows, cells), f32),
+            pltpu.VMEM((cells, cells), f32),
+            pltpu.VMEM((cells, cells), f32),
+            pltpu.VMEM((rows * cells, cells), f32),
+            pltpu.VMEM((rows, cells), f32),
+            pltpu.VMEM((2, rows, cells), f32),
+            pltpu.VMEM((n_tgt, 2, rows, cells), f32),
+            pltpu.VMEM((n_src, 2, cells), f32),
+            pltpu.VMEM((n_src, 2, cells), f32),
+            dma((3, n_src)),
+            dma((3, n_src)),
+            dma((n_tgt,)),
+            dma((n_tgt,)),
+            dma((n_src,)),
+            dma((n_src,)),
+        ],
+        compiler_params=pltpu.CompilerParams(
+            collective_id=0, has_side_effects=True, vmem_limit_bytes=48 * 1024 * 1024
+        ),
+        name="sinkhorn",
+    )(source_feat, target_feat, log_mass_src, log_mass_tgt, potential_tgt, support, counts)
+
+
+def per_device(
+    source_feat, target_feat, log_mass_src, log_mass_tgt, potential_tgt, support, counts
+):
+    rows, feats, cells = source_feat.shape
+    n_src = lax.axis_size("src")
+    dense = 4 * n_src * rows * cells * cells
+    fits = (
+        dense <= DENSE_BYTES
+        and target_feat.shape[0] == 1
+        and cells % 128 == 0
+        and rows <= cells
+        and 2 * feats == cells
+        and n_src % 8 == 0
+        and rows % 8 == 0
+    )
+    path = dense_path if fits else general_path
+    return path(
+        source_feat, target_feat, log_mass_src, log_mass_tgt, potential_tgt, support, counts
+    )
+
+
 def solution(mesh):
     in_specs = (
         P(("grp", "src"), None, None),

time: 178 us -> 31.8 us (0.18)
  blocking collectives: 110 us -> 0 us
  matrix products: 37.3 us -> 0 us
  Pallas kernels: 0 us -> 26.5 us
  local copies, waits for them, and re-layouts: 19.9 us -> 4.35 us
  other arithmetic: 8.98 us -> 0 us
    all_gather x5 -> x0, blocking collectives: 73.6 us -> none  [the longest x1 31 us: per_device(): lax.all_gather(target_feat, 'src', axis=0, tiled=True)]
    dot_general x8 -> x0, matrix products: 37.3 us -> none  [cost_tiles(): jnp.einsum('...fi,...fj->...ij', source_blk, target_blk, precision=lax.Pr...]
    pallas_call x0 -> x1, Pallas kernels: none -> 26.5 us  [dense_path(): pl.pallas_call(functools.partial(sinkhorn_kernel, n_src, n_tgt, math.gcd(...]
    pmax x1 -> x0, blocking collectives: 19.1 us -> none  [per_device(): highest = lax.pmax(best, 'src')]
    psum x1 -> x0, blocking collectives: 17.1 us -> none  [per_device(): whole = lax.psum(summed * jnp.exp(best - highest), 'src')]
    gather x25 -> x0, local copies, waits for them, and re-layouts: 14.8 us -> none  [the longest x8 4.59 us: row_pass(): return row_stats(cost, mass_all[ids_here], poten_all[ids_here], use_here)]
    reduce_sum x10 -> x0, other arithmetic: 3.79 us -> none  [the longest x4 1.49 us: column_stats(): total = jnp.sum(jnp.exp(scores - peak[:, :, None, :]), axis=2)]
    unnamed x4 -> x16, local copies, waits for them, and re-layouts: 1.28 us -> 4.35 us
where the time goes in v1:
time: 31.8 us; the launch traced here: 31.5 us
  Pallas kernels  26.5 us (83%)
  local copies, waits for them, and re-layouts  4.35 us (14%)
  between operations  0.66 us (2%)
    pallas_call x1, Pallas kernels, dense_path(): pl.pallas_call(functools.partial(sinkhorn_kernel, n_src, n_tgt, math.gcd(...  26.5 us
    unnamed x16, local copies, waits for them, and re-layouts  4.35 us

profile of v1, /device:TPU:0, one launch (start us, length us, event | category | flops | bytes accessed | tf_op | source)
XLA Modules:
  0.0 31.5 jit_solution(17631840199989554780)
XLA Ops:
  0.6 0.0 copy-start.5
  0.6 0.0 copy-start.2
  0.7 0.8 %copy.9.sup_ref = s32[16,1,8]{2,1,0:T(1,128)S(1)} copy(s32[16,1,8]{0,2,1:T(8,128)} %param.12) | data formatting | bytes 1024 | tf_op args[5]
  1.4 0.0 copy-done.5
  1.4 0.0 copy-start.3
  1.4 0.0 copy-start.4
  1.4 0.1 copy.10.cnt_ref
  1.5 0.0 copy-done.2
  1.5 0.6 %copy-done.3 = f32[1,128]{1,0:T(1,128)S(1)} copy-done((f32[1,128]{1,0:T(1,128)S(1)}, f32[1,128]{1,0:T(1,128)}, u32[]{:S(2)}) %copy-start.3) | copy-done | bytes 536
  2.1 0.0 copy-done.4
  2.1 0.0 copy-start
  2.1 1.0 %copy-done = f32[16,64,128]{2,1,0:T(8,128)S(1)} copy-done((f32[16,64,128]{2,1,0:T(8,128)S(1)}, f32[16,64,128]{2,1,0:T(8,128)}, u32[]{:S(2)}) %copy-start) | copy-done | bytes 524312
  3.1 0.0 copy-start.1
  3.1 0.8 %copy-done.1 = f32[1,64,128]{2,1,0:T(8,128)S(1)} copy-done((f32[1,64,128]{2,1,0:T(8,128)S(1)}, f32[1,64,128]{2,1,0:T(8,128)}, u32[]{:S(2)}) %copy-start.1) | copy-done | bytes 32792
  3.9 26.5 %sinkhorn.1 = (f32[16,128]{1,0:T(8,128)S(1)}, f32[1,128]{1,0:T(1,128)S(1)}) custom-call(f32[16,64,128]{2,1,0:T(8,128)S(1)} %copy-done, f32[1,64,128]{2,1,0:T(8,128)S(1)} %copy-done.1, f32[16,128]{1,0:T(8,128)S(1)} %copy-done.2, f32[1,128]{1,0:T(1,128)S(1)} %copy-done.3, f32[1,128]{1,0:T(1,128)S(1)} %copy-done.4, s32[16,1,8]{2,1,0:T(1,128)S(1)} %copy.9.sup_ref, ...), custom_call_target="tpu_custom_call" | custom-call | tf_op jit(solution)/shard_map/sinkhorn/pallas_call | solution.py:382
  30.4 0.6 %copy.13 = f32[16,128]{1,0:T(8,128)} copy(f32[16,128]{1,0:T(8,128)S(1)} %get-tuple-element.4) | data formatting | bytes 16384
  31.0 0.5 %copy.14 = f32[1,128]{1,0:T(1,128)} copy(f32[1,128]{1,0:T(1,128)S(1)} %get-tuple-element.5) | data formatting | bytes 1024
Async XLA Ops:
  0.6 0.8 %copy-start.5 = (s32[16,1]{0,1:T(1,128)S(1)}, s32[16,1]{0,1:T(1,128)}, u32[]{:S(2)}) copy-start(s32[16,1]{0,1:T(1,128)} %param.13) | copy-start | bytes 196
  0.6 0.9 %copy-start.2 = (f32[16,128]{1,0:T(8,128)S(1)}, f32[16,128]{1,0:T(8,128)}, u32[]{:S(2)}) copy-start(f32[16,128]{1,0:T(8,128)} %lms_ref.1) | copy-start | bytes 24580
  1.4 0.7 %copy-start.3 = (f32[1,128]{1,0:T(1,128)S(1)}, f32[1,128]{1,0:T(1,128)}, u32[]{:S(2)}) copy-start(f32[1,128]{1,0:T(1,128)} %lmt_ref.1) | copy-start | bytes 1540
  1.4 0.7 %copy-start.4 = (f32[1,128]{1,0:T(1,128)S(1)}, f32[1,128]{1,0:T(1,128)}, u32[]{:S(2)}) copy-start(f32[1,128]{1,0:T(1,128)} %pt_ref.1) | copy-start | bytes 1540
  2.1 1.0 %copy-start = (f32[16,64,128]{2,1,0:T(8,128)S(1)}, f32[16,64,128]{2,1,0:T(8,128)}, u32[]{:S(2)}) copy-start(f32[16,64,128]{2,1,0:T(8,128)} %x_ref.1) | copy-start | bytes 1572868
  3.1 0.8 %copy-start.1 = (f32[1,64,128]{2,1,0:T(8,128)S(1)}, f32[1,64,128]{2,1,0:T(8,128)}, u32[]{:S(2)}) copy-start(f32[1,64,128]{2,1,0:T(8,128)} %y_ref.1) | copy-start | bytes 98308

commit v2 on v1

--- a/solution.py
+++ b/solution.py
@@ -165,15 +165,16 @@
 
 
 def sinkhorn_kernel(
-    n_src, n_tgt, chunk,
-    x_ref, y_ref, lms_ref, lmt_ref, pt_ref, sup_ref, cnt_ref,
+    n_src, n_tgt, group,
+    x_hbm, y_hbm, lms_hbm, lmt_hbm, pt_hbm, sup_hbm, cnt_hbm,
     ps_ref, pn_ref,
-    y_all, lm_all, pt_all, xt, scores, run_max, bias, peak_col, total_col, shift,
+    x_ref, lms_ref, sup_ref, cnt_ref,
+    y_all, lm_all, pt_all, xt, scores, run_max, square, used, stat_col, shift,
     x_sq, stat_out, stat_in, col_out, col_in,
-    y_send, y_recv, s_send, s_recv, c_send, c_recv,
+    local, y_send, y_recv, s_send, s_recv, c_send, c_recv,
 ):
     rows, feats, cells = x_ref.shape
-    slots = sup_ref.shape[2]
+    slots = sup_ref.shape[1]
     grp = lax.axis_index("grp")
     me = lax.axis_index("src")
     shard = lax.axis_index("tgt")
@@ -187,9 +188,25 @@
         pl.semaphore_signal(
             barrier, inc=1, device_id=(grp, me, (shard + step) % n_tgt), device_id_type=MESH
         )
+    fetches = [
+        pltpu.make_async_copy(here, there, local.at[index])
+        for index, (here, there) in enumerate(
+            (
+                (x_hbm, x_ref),
+                (sup_hbm, sup_ref),
+                (cnt_hbm, cnt_ref),
+                (lms_hbm, lms_ref),
+                (y_hbm, y_all.at[pl.ds(me, 1)]),
+                (lmt_hbm, lm_all.at[pl.ds(me, 1)]),
+                (pt_hbm, pt_all.at[pl.ds(me, 1)]),
+            )
+        )
+    ]
+    for fetch in fetches:
+        fetch.start()
     pl.semaphore_wait(barrier, n_src - 1 + n_tgt - 1)
 
-    parts = ((y_ref, y_all), (lmt_ref, lm_all), (pt_ref, pt_all))
+    parts = ((y_hbm, y_all), (lmt_hbm, lm_all), (pt_hbm, pt_all))
 
     def target_copy(index, where, step, peer):
         mine, everyone = parts[index]
@@ -206,9 +223,8 @@
         peer = partner(me, step, n_src)
         for index in range(3):
             target_copy(index, me, step, peer).start()
-    y_all[me] = y_ref[0]
-    lm_all[pl.ds(me, 1)] = lmt_ref[...]
-    pt_all[pl.ds(me, 1)] = pt_ref[...]
+    for fetch in fetches:
+        fetch.wait()
 
     def prepare(row, carry):
         x = x_ref[row]
@@ -226,9 +242,16 @@
     run_max[...] = jnp.full(run_max.shape, 4.0 * very_low, jnp.float32)
 
     limits = cnt_ref[...]
-    ids = sup_ref[:, 0, :]
-
-    def block_scores(block):
+    names = lax.broadcasted_iota(jnp.int32, (n_src, rows), 0)
+    joined = jnp.zeros((n_src, rows), jnp.bool_)
+    for slot in range(slots):
+        joined = joined | ((sup_ref[0, slot : slot + 1] == names) & (limits > slot))
+    square[...] = jnp.zeros_like(square)
+    square[0:n_src, 0:rows] = jnp.where(joined, 0.0, very_low)
+    used[...] = square[...].T[:rows]
+    row_lanes = lax.broadcasted_iota(jnp.int32, (rows, cells), 1)
+
+    def operand(block):
         y = y_all[block]
         high, mid, low = split3(y)
         weights = jnp.concatenate([high, high, mid, mid, high, low], axis=0).astype(jnp.bfloat16)
@@ -236,51 +259,67 @@
         level = LOG2E * (
             lm_all[pl.ds(block, 1)] + 2.0 * pt_all[pl.ds(block, 1)] - 2.0 * y_sq
         )
-        joined = jnp.zeros((rows, 1), jnp.bool_)
-        for slot in range(slots):
-            joined = joined | ((ids[:, slot : slot + 1] == block) & (limits > slot))
-        bias[...] = level + jnp.where(joined, 0.0, very_low)
-        for start in range(0, rows, chunk):
-            here = slice(start * cells, (start + chunk) * cells)
+        closed = jnp.sum(jnp.where(row_lanes == block, used[...], 0.0), axis=1, keepdims=True)
+        return weights, level + closed
+
+    def block_scores(blocks):
+        pairs = [operand(block) for block in blocks]
+        weights = jnp.concatenate([pair[0] for pair in pairs], axis=1)
+        for start in range(0, rows, group):
+            here = slice(start * cells, (start + group) * cells)
             cross = jnp.dot(xt[here, :], weights, preferred_element_type=jnp.float32)
-            for row in range(chunk):
+            for row in range(group):
                 tile = slice((start + row) * cells, (start + row + 1) * cells)
-                value = cross[row * cells : (row + 1) * cells] + bias[start + row : start + row + 1]
-                scores[block, tile] = value
-                run_max[tile] = jnp.maximum(run_max[tile], value)
-
-    block_scores(me)
-
-    def arrival(step, carry):
+                best = run_max[tile]
+                for place, block in enumerate(blocks):
+                    value = (
+                        cross[row * cells : (row + 1) * cells, place * cells : (place + 1) * cells]
+                        + pairs[place][1][start + row : start + row + 1]
+                    )
+                    scores[block, tile] = value
+                    best = jnp.maximum(best, value)
+                run_max[tile] = best
+
+    def await_block(step):
         block = origin(me, step, n_src)
         for index in range(3):
             target_copy(index, block, step, block).wait_recv()
-        block_scores(block)
+        return block
+
+    block_scores((me, await_block(1)))
+
+    def arrival(index, carry):
+        block_scores((await_block(2 * index), await_block(2 * index + 1)))
         return carry
 
-    lax.fori_loop(1, n_src, arrival, 0)
+    lax.fori_loop(1, n_src // 2, arrival, 0)
 
     lanes = lax.broadcasted_iota(jnp.int32, (cells, cells), 1)
-    peak_col[...] = jnp.zeros_like(peak_col)
-    total_col[...] = jnp.ones_like(total_col)
-
-    def row_block(row, carry):
+    stat_col[...] = jnp.zeros_like(stat_col)
+
+    def row_block(row):
         here = pl.ds(row * cells, cells)
         peak = jnp.max(run_max[here], axis=1, keepdims=True)
         gathered = jnp.exp2(scores[0, here] - peak)
         for block in range(1, n_src):
             gathered = gathered + jnp.exp2(scores[block, here] - peak)
         total = jnp.sum(gathered, axis=1, keepdims=True)
-        chosen = lanes == row
-        peak_col[...] = jnp.where(chosen, peak, peak_col[...])
-        total_col[...] = jnp.where(chosen, total, total_col[...])
+        return peak, total
+
+    def row_group(index, carry):
+        filled = stat_col[...]
+        for place in range(group):
+            row = index * group + place
+            peak, total = row_block(row)
+            filled = jnp.where(lanes == row, peak, filled)
+            filled = jnp.where(lanes == rows + row, total, filled)
+        stat_col[...] = filled
         return carry
 
-    lax.fori_loop(0, rows, row_block, 0)
-    own_peak = peak_col[...].T[:rows]
-    own_total = total_col[...].T[:rows]
-    stat_out[0] = own_peak
-    stat_out[1] = own_total
+    lax.fori_loop(0, rows // group, row_group, 0)
+    stats = stat_col[...].T[: 2 * rows]
+    own_peak, own_total = stats[:rows], stats[rows:]
+    stat_out[...] = stats
 
     def stat_copy(where, step, peer):
         return pltpu.make_async_remote_copy(
@@ -301,7 +340,7 @@
         stat_copy(step, step, (shard + step) % n_tgt).wait_recv()
     peak, total = own_peak, own_total
     for step in range(1, n_tgt):
-        other_peak, other_total = stat_in[step, 0], stat_in[step, 1]
+        other_peak, other_total = stat_in[step, 0:rows], stat_in[step, rows : 2 * rows]
         highest = jnp.maximum(peak, other_peak)
         total = total * jnp.exp2(peak - highest) + other_total * jnp.exp2(other_peak - highest)
         peak = highest
@@ -315,21 +354,25 @@
         )
 
     def column(block):
-        def highest(row, best):
-            here = pl.ds(row * cells, cells)
+        many = 2 * group
+        pieces = many * cells // 8
+
+        def highest(index, best):
+            here = pl.ds(index * many * cells, many * cells)
             value = scores[block, here] + shift[here]
             scores[block, here] = value
-            return jnp.maximum(best, jnp.max(value.reshape(cells // 8, 8, cells), axis=0))
-
-        best = lax.fori_loop(0, rows, highest, jnp.full((8, cells), 4.0 * very_low, jnp.float32))
+            return jnp.maximum(best, jnp.max(value.reshape(pieces, 8, cells), axis=0))
+
+        best = jnp.full((8, cells), 4.0 * very_low, jnp.float32)
+        best = lax.fori_loop(0, rows // many, highest, best)
         best = jnp.max(best, axis=0, keepdims=True)
 
-        def add(row, summed):
-            here = pl.ds(row * cells, cells)
+        def add(index, summed):
+            here = pl.ds(index * many * cells, many * cells)
             value = jnp.exp2(scores[block, here] - best)
-            return summed + jnp.sum(value.reshape(cells // 8, 8, cells), axis=0)
-
-        summed = lax.fori_loop(0, rows, add, jnp.zeros((8, cells), jnp.float32))
+            return summed + jnp.sum(value.reshape(pieces, 8, cells), axis=0)
+
+        summed = lax.fori_loop(0, rows // many, add, jnp.zeros((8, cells), jnp.float32))
         return best, jnp.sum(summed, axis=0, keepdims=True)
 
     def column_copy(dest, where, step):
@@ -363,8 +406,8 @@
     highest = jnp.max(peaks, axis=0, keepdims=True)
     whole = jnp.sum(totals * jnp.exp2(peaks - highest), axis=0, keepdims=True)
     pn_ref[...] = (
-        pt_ref[...]
-        + entropic * lmt_ref[...]
+        pt_all[pl.ds(me, 1)]
+        + entropic * lm_all[pl.ds(me, 1)]
         - (entropic * LN2) * (highest + jnp.log(whole) * LOG2E)
     )
     for step in range(1, n_tgt):
@@ -379,30 +422,37 @@
     vmem = pl.BlockSpec(memory_space=pltpu.VMEM)
     f32 = jnp.float32
     dma = pltpu.SemaphoreType.DMA
+    lists = jnp.transpose(support, (1, 2, 0))
+    limits = counts.T
     return pl.pallas_call(
-        functools.partial(sinkhorn_kernel, n_src, n_tgt, math.gcd(rows, 4)),
+        functools.partial(sinkhorn_kernel, n_src, n_tgt, 4),
         out_shape=(
             jax.ShapeDtypeStruct((rows, cells), f32),
             jax.ShapeDtypeStruct((1, cells), f32),
         ),
-        in_specs=[vmem] * 7,
+        in_specs=[pl.BlockSpec(memory_space=pl.ANY)] * 7,
         out_specs=(vmem, vmem),
         scratch_shapes=[
+            pltpu.VMEM(source_feat.shape, f32),
+            pltpu.VMEM((rows, cells), f32),
+            pltpu.VMEM(lists.shape, jnp.int32),
+            pltpu.VMEM(limits.shape, jnp.int32),
             pltpu.VMEM((n_src, feats, cells), f32),
             pltpu.VMEM((n_src, cells), f32),
             pltpu.VMEM((n_src, cells), f32),
             pltpu.VMEM((rows * cells, 6 * feats), jnp.bfloat16),
             pltpu.VMEM((n_src, rows * cells, cells), f32),
             pltpu.VMEM((rows * cells, cells), f32),
+            pltpu.VMEM((cells, cells), f32),
             pltpu.VMEM((rows, cells), f32),
-            pltpu.VMEM((cells, cells), f32),
             pltpu.VMEM((cells, cells), f32),
             pltpu.VMEM((rows * cells, cells), f32),
             pltpu.VMEM((rows, cells), f32),
-            pltpu.VMEM((2, rows, cells), f32),
-            pltpu.VMEM((n_tgt, 2, rows, cells), f32),
+            pltpu.VMEM((2 * rows, cells), f32),
+            pltpu.VMEM((n_tgt, 2 * rows, cells), f32),
             pltpu.VMEM((n_src, 2, cells), f32),
             pltpu.VMEM((n_src, 2, cells), f32),
+            dma((7,)),
             dma((3, n_src)),
             dma((3, n_src)),
             dma((n_tgt,)),
@@ -411,10 +461,10 @@
             dma((n_src,)),
         ],
         compiler_params=pltpu.CompilerParams(
-            collective_id=0, has_side_effects=True, vmem_limit_bytes=48 * 1024 * 1024
+            collective_id=0, has_side_effects=True, vmem_limit_bytes=60 * 1024 * 1024
         ),
         name="sinkhorn",
-    )(source_feat, target_feat, log_mass_src, log_mass_tgt, potential_tgt, support, counts)
+    )(source_feat, target_feat, log_mass_src, log_mass_tgt, potential_tgt, lists, limits)
 
 
 def per_device(
@@ -427,7 +477,7 @@
         dense <= DENSE_BYTES
         and target_feat.shape[0] == 1
         and cells % 128 == 0
-        and rows <= cells
+        and 2 * rows <= cells
         and 2 * feats == cells
         and n_src % 8 == 0
         and rows % 8 == 0

time: 31.8 us -> 26.8 us (0.84)
  local copies, waits for them, and re-layouts: 4.35 us -> 1.81 us
  Pallas kernels: 26.5 us -> 24.2 us
    unnamed x16 -> x4, local copies, waits for them, and re-layouts: 4.35 us -> 1.81 us
    pallas_call x1, Pallas kernels: 26.5 us -> 24.2 us  [dense_path(): pl.pallas_call(functools.partial(sinkhorn_kernel, n_src, n_tgt, 4), out_s...]
where the time goes in v2:
time: 26.8 us; the launch traced here: 26.6 us
  Pallas kernels  24.2 us (90%)
  local copies, waits for them, and re-layouts  1.81 us (7%)
  between operations  0.65 us (2%)
    pallas_call x1, Pallas kernels, dense_path(): pl.pallas_call(functools.partial(sinkhorn_kernel, n_src, n_tgt, 4), out_s...  24.2 us
    unnamed x4, local copies, waits for them, and re-layouts  1.81 us

profile of v2, /device:TPU:0, one launch (start us, length us, event | category | flops | bytes accessed | tf_op | source)
XLA Modules:
  0.0 26.6 jit_solution(14247261933749303856)
XLA Ops:
  0.6 24.2 %sinkhorn.1 = (f32[16,128]{1,0:T(8,128)}, f32[1,128]{1,0:T(1,128)}) custom-call(f32[16,64,128]{2,1,0:T(8,128)} %x_hbm.1, f32[1,64,128]{2,1,0:T(8,128)} %y_hbm.1, f32[16,128]{1,0:T(8,128)} %lms_hbm.1, f32[1,128]{1,0:T(1,128)} %lmt_hbm.1, f32[1,128]{1,0:T(1,128)} %pt_hbm.1, s32[1,8,16]{2,1,0:T(8,128)} %bitcast.2, s32[1,16]{1,0:T(1,128)} %bitcast.3), custom_call_target="tpu_custom_call" | custom-call | tf_op jit(solution)/shard_map/sinkhorn/pallas_call | solution.py:427
  24.8 0.0 copy-start
  24.8 1.3 %copy.11 = f32[16,128]{1,0:T(8,128)} copy(f32[16,128]{1,0:T(8,128)} %get-tuple-element.4) | data formatting | bytes 16384
  26.1 0.0 copy-done
  26.1 0.5 %copy.12 = f32[1,128]{1,0:T(1,128)} copy(f32[1,128]{1,0:T(1,128)S(1)} %copy-done) | data formatting | bytes 1024
Async XLA Ops:
  24.8 1.3 %copy-start = (f32[1,128]{1,0:T(1,128)S(1)}, f32[1,128]{1,0:T(1,128)}, u32[]{:S(2)}) copy-start(f32[1,128]{1,0:T(1,128)} %get-tuple-element.5) | copy-start | bytes 1540

commit v3 on v2

--- a/solution.py
+++ b/solution.py
@@ -169,7 +169,7 @@
     x_hbm, y_hbm, lms_hbm, lmt_hbm, pt_hbm, sup_hbm, cnt_hbm,
     ps_ref, pn_ref,
     x_ref, lms_ref, sup_ref, cnt_ref,
-    y_all, lm_all, pt_all, xt, scores, run_max, square, used, stat_col, shift,
+    y_all, lm_all, pt_all, xt, scores, square, used, stat_col, shift,
     x_sq, stat_out, stat_in, col_out, col_in,
     local, y_send, y_recv, s_send, s_recv, c_send, c_recv,
 ):
@@ -239,7 +239,6 @@
         return carry
 
     lax.fori_loop(0, rows, prepare, 0)
-    run_max[...] = jnp.full(run_max.shape, 4.0 * very_low, jnp.float32)
 
     limits = cnt_ref[...]
     names = lax.broadcasted_iota(jnp.int32, (n_src, rows), 0)
@@ -262,23 +261,33 @@
         closed = jnp.sum(jnp.where(row_lanes == block, used[...], 0.0), axis=1, keepdims=True)
         return weights, level + closed
 
-    def block_scores(blocks):
+    lanes = lax.broadcasted_iota(jnp.int32, (cells, cells), 1)
+    stat_col[...] = jnp.zeros_like(stat_col)
+
+    def block_scores(turn, blocks):
         pairs = [operand(block) for block in blocks]
         weights = jnp.concatenate([pair[0] for pair in pairs], axis=1)
+        filled = stat_col[...]
         for start in range(0, rows, group):
             here = slice(start * cells, (start + group) * cells)
             cross = jnp.dot(xt[here, :], weights, preferred_element_type=jnp.float32)
-            for row in range(group):
-                tile = slice((start + row) * cells, (start + row + 1) * cells)
-                best = run_max[tile]
-                for place, block in enumerate(blocks):
-                    value = (
-                        cross[row * cells : (row + 1) * cells, place * cells : (place + 1) * cells]
-                        + pairs[place][1][start + row : start + row + 1]
-                    )
+            for part in range(group):
+                row = start + part
+                tile = slice(row * cells, (row + 1) * cells)
+                values = [
+                    cross[part * cells : (part + 1) * cells, place * cells : (place + 1) * cells]
+                    + pairs[place][1][row : row + 1]
+                    for place in range(len(blocks))
+                ]
+                for block, value in zip(blocks, values):
                     scores[block, tile] = value
-                    best = jnp.maximum(best, value)
-                run_max[tile] = best
+                peak = jnp.max(functools.reduce(jnp.maximum, values), axis=1, keepdims=True)
+                total = functools.reduce(jnp.add, [jnp.exp2(value - peak) for value in values])
+                total = jnp.sum(total, axis=1, keepdims=True)
+                lane = turn * (2 * rows) + row
+                filled = jnp.where(lanes == lane, peak, filled)
+                filled = jnp.where(lanes == lane + rows, total, filled)
+        stat_col[...] = filled
 
     def await_block(step):
         block = origin(me, step, n_src)
@@ -286,40 +295,29 @@
             target_copy(index, block, step, block).wait_recv()
         return block
 
-    block_scores((me, await_block(1)))
+    block_scores(0, (me, await_block(1)))
 
     def arrival(index, carry):
-        block_scores((await_block(2 * index), await_block(2 * index + 1)))
+        block_scores(index, (await_block(2 * index), await_block(2 * index + 1)))
         return carry
 
     lax.fori_loop(1, n_src // 2, arrival, 0)
 
-    lanes = lax.broadcasted_iota(jnp.int32, (cells, cells), 1)
-    stat_col[...] = jnp.zeros_like(stat_col)
-
-    def row_block(row):
-        here = pl.ds(row * cells, cells)
-        peak = jnp.max(run_max[here], axis=1, keepdims=True)
-        gathered = jnp.exp2(scores[0, here] - peak)
-        for block in range(1, n_src):
-            gathered = gathered + jnp.exp2(scores[block, here] - peak)
-        total = jnp.sum(gathered, axis=1, keepdims=True)
-        return peak, total
-
-    def row_group(index, carry):
-        filled = stat_col[...]
-        for place in range(group):
-            row = index * group + place
-            peak, total = row_block(row)
-            filled = jnp.where(lanes == row, peak, filled)
-            filled = jnp.where(lanes == rows + row, total, filled)
-        stat_col[...] = filled
-        return carry
-
-    lax.fori_loop(0, rows // group, row_group, 0)
-    stats = stat_col[...].T[: 2 * rows]
-    own_peak, own_total = stats[:rows], stats[rows:]
-    stat_out[...] = stats
+    def joined_stats(first, second):
+        highest = jnp.maximum(first[0], second[0])
+        summed = first[1] * jnp.exp2(first[0] - highest) + second[1] * jnp.exp2(second[0] - highest)
+        return highest, summed
+
+    stats = stat_col[...].T
+    turns = [
+        (stats[2 * rows * turn :][:rows], stats[2 * rows * turn + rows :][:rows])
+        for turn in range(n_src // 2)
+    ]
+    while len(turns) > 1:
+        turns = [joined_stats(*turns[place : place + 2]) for place in range(0, len(turns), 2)]
+    own_peak, own_total = turns[0]
+    stat_out[0:rows] = own_peak
+    stat_out[rows : 2 * rows] = own_total
 
     def stat_copy(where, step, peer):
         return pltpu.make_async_remote_copy(
@@ -340,10 +338,8 @@
         stat_copy(step, step, (shard + step) % n_tgt).wait_recv()
     peak, total = own_peak, own_total
     for step in range(1, n_tgt):
-        other_peak, other_total = stat_in[step, 0:rows], stat_in[step, rows : 2 * rows]
-        highest = jnp.maximum(peak, other_peak)
-        total = total * jnp.exp2(peak - highest) + other_total * jnp.exp2(other_peak - highest)
-        peak = highest
+        other = (stat_in[step, 0:rows], stat_in[step, rows : 2 * rows])
+        peak, total = joined_stats((peak, total), other)
     joint = peak + jnp.log(total) * LOG2E
     ps_ref[...] = x_sq[...] - (entropic * LN2) * joint
     offset = LOG2E * lms_ref[...] - joint
@@ -353,27 +349,27 @@
             offset[:, row : row + 1], (cells, cells)
         )
 
-    def column(block):
-        many = 2 * group
-        pieces = many * cells // 8
-
-        def highest(index, best):
-            here = pl.ds(index * many * cells, many * cells)
-            value = scores[block, here] + shift[here]
-            scores[block, here] = value
-            return jnp.maximum(best, jnp.max(value.reshape(pieces, 8, cells), axis=0))
-
-        best = jnp.full((8, cells), 4.0 * very_low, jnp.float32)
-        best = lax.fori_loop(0, rows // many, highest, best)
-        best = jnp.max(best, axis=0, keepdims=True)
-
-        def add(index, summed):
-            here = pl.ds(index * many * cells, many * cells)
-            value = jnp.exp2(scores[block, here] - best)
-            return summed + jnp.sum(value.reshape(pieces, 8, cells), axis=0)
-
-        summed = lax.fori_loop(0, rows // many, add, jnp.zeros((8, cells), jnp.float32))
-        return best, jnp.sum(summed, axis=0, keepdims=True)
+    many = 2 * group
+    pieces = many * cells // 8
+    lowest = jnp.full((8, cells), 4.0 * very_low, jnp.float32)
+    nothing = jnp.zeros((8, cells), jnp.float32)
+
+    def find(block, here, best):
+        value = scores[block, here] + shift[here]
+        return jnp.maximum(best, jnp.max(value.reshape(pieces, 8, cells), axis=0))
+
+    def add(block, here, best, summed):
+        value = jnp.exp2(scores[block, here] + shift[here] - best)
+        return summed + jnp.sum(value.reshape(pieces, 8, cells), axis=0)
+
+    def span(index):
+        return pl.ds(index * many * cells, many * cells)
+
+    def whole_column(summed):
+        return jnp.sum(summed, axis=0, keepdims=True)
+
+    def peak_of(best):
+        return jnp.max(best, axis=0, keepdims=True)
 
     def column_copy(dest, where, step):
         return pltpu.make_async_remote_copy(
@@ -385,17 +381,28 @@
             device_id_type=MESH,
         )
 
-    def send_column(index, carry):
+    def send_column(index, best):
         step = n_src - 1 - index
         block = partner(me, step, n_src)
-        best, summed = column(block)
+        following = partner(me, step - 1, n_src)
+        summed, later = nothing, lowest
+        for part in range(rows // many):
+            summed = add(block, span(part), best, summed)
+            later = find(following, span(part), later)
         col_out[block, 0:1] = best
-        col_out[block, 1:2] = summed
+        col_out[block, 1:2] = whole_column(summed)
         column_copy(block, me, step).start()
-        return carry
-
-    lax.fori_loop(0, n_src - 1, send_column, 0)
-    best, summed = column(me)
+        return peak_of(later)
+
+    farthest = partner(me, n_src - 1, n_src)
+    best = lowest
+    for part in range(rows // many):
+        best = find(farthest, span(part), best)
+    best = lax.fori_loop(0, n_src - 1, send_column, peak_of(best))
+    summed = nothing
+    for part in range(rows // many):
+        summed = add(me, span(part), best, summed)
+    summed = whole_column(summed)
     col_in[me, 0:1] = best
     col_in[me, 1:2] = summed
     for step in range(1, n_src):
@@ -442,7 +449,6 @@
             pltpu.VMEM((n_src, cells), f32),
             pltpu.VMEM((rows * cells, 6 * feats), jnp.bfloat16),
             pltpu.VMEM((n_src, rows * cells, cells), f32),
-            pltpu.VMEM((rows * cells, cells), f32),
             pltpu.VMEM((cells, cells), f32),
             pltpu.VMEM((rows, cells), f32),
             pltpu.VMEM((cells, cells), f32),
@@ -477,7 +483,9 @@
         dense <= DENSE_BYTES
         and target_feat.shape[0] == 1
         and cells % 128 == 0
-        and 2 * rows <= cells
+        and n_src * rows <= cells
+        and rows % 8 == 0
+        and not (n_src // 2) & (n_src // 2 - 1)
         and 2 * feats == cells
         and n_src % 8 == 0
         and rows % 8 == 0

time: 26.8 us -> 24.5 us (0.914)
  Pallas kernels: 24.2 us -> 21.9 us
    pallas_call x1, Pallas kernels: 24.2 us -> 21.9 us  [dense_path(): pl.pallas_call(functools.partial(sinkhorn_kernel, n_src, n_tgt, 4), out_s...]
where the time goes in v3:
time: 24.5 us; the launch traced here: 24.3 us
  Pallas kernels  21.9 us (89%)
  local copies, waits for them, and re-layouts  1.81 us (7%)
  between operations  0.65 us (3%)
    pallas_call x1, Pallas kernels, dense_path(): pl.pallas_call(functools.partial(sinkhorn_kernel, n_src, n_tgt, 4), out_s...  21.9 us
    unnamed x4, local copies, waits for them, and re-layouts  1.81 us

profile of v3, /device:TPU:0, one launch (start us, length us, event | category | flops | bytes accessed | tf_op | source)
XLA Modules:
  0.0 24.3 jit_solution(4197774607314038075)
XLA Ops:
  0.6 21.9 %sinkhorn.1 = (f32[16,128]{1,0:T(8,128)}, f32[1,128]{1,0:T(1,128)}) custom-call(f32[16,64,128]{2,1,0:T(8,128)} %x_hbm.1, f32[1,64,128]{2,1,0:T(8,128)} %y_hbm.1, f32[16,128]{1,0:T(8,128)} %lms_hbm.1, f32[1,128]{1,0:T(1,128)} %lmt_hbm.1, f32[1,128]{1,0:T(1,128)} %pt_hbm.1, s32[1,8,16]{2,1,0:T(8,128)} %bitcast.2, s32[1,16]{1,0:T(1,128)} %bitcast.3), custom_call_target="tpu_custom_call" | custom-call | tf_op jit(solution)/shard_map/sinkhorn/pallas_call | solution.py:434
  22.5 0.0 copy-start
  22.5 1.3 %copy.11 = f32[16,128]{1,0:T(8,128)} copy(f32[16,128]{1,0:T(8,128)} %get-tuple-element.4) | data formatting | bytes 16384
  23.8 0.0 copy-done
  23.8 0.5 %copy.12 = f32[1,128]{1,0:T(1,128)} copy(f32[1,128]{1,0:T(1,128)S(1)} %copy-done) | data formatting | bytes 1024
Async XLA Ops:
  22.5 1.3 %copy-start = (f32[1,128]{1,0:T(1,128)S(1)}, f32[1,128]{1,0:T(1,128)}, u32[]{:S(2)}) copy-start(f32[1,128]{1,0:T(1,128)} %get-tuple-element.5) | copy-start | bytes 1540

commit v4 on v3

--- a/solution.py
+++ b/solution.py
@@ -149,19 +149,11 @@
 
 
 def partner(me, step, count):
-    if count & (count - 1):
-        return (me + step) % count
     met, bit = 0, 1
     while bit < count:
         met = met + bit * ((me // bit + step // bit) % 2)
         bit *= 2
     return met
-
-
-def origin(me, step, count):
-    if count & (count - 1):
-        return (me - step + count) % count
-    return partner(me, step, count)
 
 
 def sinkhorn_kernel(
@@ -219,10 +211,23 @@
             device_id_type=MESH,
         )
 
+    def relay(step):
+        block = partner(me, step, n_src)
+        return pltpu.make_async_remote_copy(
+            src_ref=y_all.at[pl.ds(block, 1)],
+            dst_ref=y_all.at[pl.ds(block, 1)],
+            send_sem=y_send.at[0, step + 1],
+            recv_sem=y_recv.at[0, block],
+            device_id=(grp, partner(me, 1, n_src), shard),
+            device_id_type=MESH,
+        )
+
+    far_steps = range(n_src - 2, 0, -2)
+    for step in (1, *far_steps):
+        target_copy(0, me, step, partner(me, step, n_src)).start()
     for step in range(1, n_src):
-        peer = partner(me, step, n_src)
-        for index in range(3):
-            target_copy(index, me, step, peer).start()
+        for index in (1, 2):
+            target_copy(index, me, step, partner(me, step, n_src)).start()
     for fetch in fetches:
         fetch.wait()
 
@@ -289,16 +294,26 @@
                 filled = jnp.where(lanes == lane + rows, total, filled)
         stat_col[...] = filled
 
-    def await_block(step):
-        block = origin(me, step, n_src)
-        for index in range(3):
-            target_copy(index, block, step, block).wait_recv()
-        return block
-
-    block_scores(0, (me, await_block(1)))
-
-    def arrival(index, carry):
-        block_scores(index, (await_block(2 * index), await_block(2 * index + 1)))
+    def await_part(index, step):
+        block = partner(me, step, n_src)
+        target_copy(index, block, step, block).wait_recv()
+
+    def await_pair(turn):
+        for index in (1, 2):
+            await_part(index, 2 * turn)
+            await_part(index, 2 * turn + 1)
+        await_part(0, 2 * turn + 1)
+        return partner(me, 2 * turn, n_src), partner(me, 2 * turn + 1, n_src)
+
+    for index in range(3):
+        await_part(index, 1)
+    block_scores(0, (me, partner(me, 1, n_src)))
+    for step in reversed(far_steps):
+        await_part(0, step)
+        relay(step).start()
+
+    def arrival(turn, carry):
+        block_scores(turn, await_pair(turn))
         return carry
 
     lax.fori_loop(1, n_src // 2, arrival, 0)
@@ -331,8 +346,12 @@
 
     for step in range(1, n_tgt):
         stat_copy(step, step, (shard + step) % n_tgt).start()
+    for step in (1, *far_steps):
+        target_copy(0, me, step, partner(me, step, n_src)).wait_send()
+    for step in far_steps:
+        relay(step).wait_send()
     for step in range(1, n_src):
-        for index in range(3):
+        for index in (1, 2):
             target_copy(index, me, step, partner(me, step, n_src)).wait_send()
     for step in range(1, n_tgt):
         stat_copy(step, step, (shard + step) % n_tgt).wait_recv()
@@ -349,7 +368,7 @@
             offset[:, row : row + 1], (cells, cells)
         )
 
-    many = 2 * group
+    many = 8
     pieces = many * cells // 8
     lowest = jnp.full((8, cells), 4.0 * very_low, jnp.float32)
     nothing = jnp.zeros((8, cells), jnp.float32)
@@ -406,7 +425,7 @@
     col_in[me, 0:1] = best
     col_in[me, 1:2] = summed
     for step in range(1, n_src):
-        sender = origin(me, step, n_src)
+        sender = partner(me, step, n_src)
         column_copy(sender, sender, step).wait_recv()
     peaks = col_in[:, 0, :]
     totals = col_in[:, 1, :]
@@ -485,7 +504,7 @@
         and cells % 128 == 0
         and n_src * rows <= cells
         and rows % 8 == 0
-        and not (n_src // 2) & (n_src // 2 - 1)
+        and not n_src & (n_src - 1)
         and 2 * feats == cells
         and n_src % 8 == 0
         and rows % 8 == 0

time: 24.5 us -> 25.5 us (1.041)
  Pallas kernels: 21.9 us -> 22.8 us
    pallas_call x1, Pallas kernels: 21.9 us -> 22.8 us  [dense_path(): pl.pallas_call(functools.partial(sinkhorn_kernel, n_src, n_tgt, 4), out_s...]
where the time goes in v4:
time: 25.5 us; the launch traced here: 25.3 us
  Pallas kernels  22.8 us (89%)
  local copies, waits for them, and re-layouts  1.81 us (7%)
  between operations  0.65 us (3%)
    pallas_call x1, Pallas kernels, dense_path(): pl.pallas_call(functools.partial(sinkhorn_kernel, n_src, n_tgt, 4), out_s...  22.8 us
    unnamed x4, local copies, waits for them, and re-layouts  1.81 us

profile of v4, /device:TPU:0, one launch (start us, length us, event | category | flops | bytes accessed | tf_op | source)
XLA Modules:
  0.0 25.3 jit_solution(5403146393666724410)
XLA Ops:
  0.6 22.8 %sinkhorn.1 = (f32[16,128]{1,0:T(8,128)}, f32[1,128]{1,0:T(1,128)}) custom-call(f32[16,64,128]{2,1,0:T(8,128)} %x_hbm.1, f32[1,64,128]{2,1,0:T(8,128)} %y_hbm.1, f32[16,128]{1,0:T(8,128)} %lms_hbm.1, f32[1,128]{1,0:T(1,128)} %lmt_hbm.1, f32[1,128]{1,0:T(1,128)} %pt_hbm.1, s32[1,8,16]{2,1,0:T(8,128)} %bitcast.2, s32[1,16]{1,0:T(1,128)} %bitcast.3), custom_call_target="tpu_custom_call" | custom-call | tf_op jit(solution)/shard_map/sinkhorn/pallas_call | solution.py:453
  23.5 0.0 copy-start
  23.5 1.3 %copy.11 = f32[16,128]{1,0:T(8,128)} copy(f32[16,128]{1,0:T(8,128)} %get-tuple-element.4) | data formatting | bytes 16384
  24.8 0.0 copy-done
  24.8 0.5 %copy.12 = f32[1,128]{1,0:T(1,128)} copy(f32[1,128]{1,0:T(1,128)S(1)} %copy-done) | data formatting | bytes 1024
Async XLA Ops:
  23.5 1.3 %copy-start = (f32[1,128]{1,0:T(1,128)S(1)}, f32[1,128]{1,0:T(1,128)}, u32[]{:S(2)}) copy-start(f32[1,128]{1,0:T(1,128)} %get-tuple-element.5) | copy-start | bytes 1540

commit v5 on v3

--- a/solution.py
+++ b/solution.py
@@ -431,13 +431,19 @@
     dma = pltpu.SemaphoreType.DMA
     lists = jnp.transpose(support, (1, 2, 0))
     limits = counts.T
+    operands = [
+        pltpu.with_memory_space_constraint(array, pltpu.HBM)
+        for array in (
+            source_feat, target_feat, log_mass_src, log_mass_tgt, potential_tgt, lists, limits
+        )
+    ]
     return pl.pallas_call(
         functools.partial(sinkhorn_kernel, n_src, n_tgt, 4),
         out_shape=(
             jax.ShapeDtypeStruct((rows, cells), f32),
             jax.ShapeDtypeStruct((1, cells), f32),
         ),
-        in_specs=[pl.BlockSpec(memory_space=pl.ANY)] * 7,
+        in_specs=[pl.BlockSpec(memory_space=pltpu.HBM)] * 7,
         out_specs=(vmem, vmem),
         scratch_shapes=[
             pltpu.VMEM(source_feat.shape, f32),
@@ -467,10 +473,10 @@
             dma((n_src,)),
         ],
         compiler_params=pltpu.CompilerParams(
-            collective_id=0, has_side_effects=True, vmem_limit_bytes=60 * 1024 * 1024
+            collective_id=0, has_side_effects=True, vmem_limit_bytes=32 * 1024 * 1024
         ),
         name="sinkhorn",
-    )(source_feat, target_feat, log_mass_src, log_mass_tgt, potential_tgt, lists, limits)
+    )(*operands)
 
 
 def per_device(

time: 24.5 us -> 23.2 us (0.947)
  local copies, waits for them, and re-layouts: 1.81 us -> 1.11 us
  Pallas kernels: 21.9 us -> 21.3 us
    unnamed x4 -> x2, local copies, waits for them, and re-layouts: 1.81 us -> 1.11 us
    pallas_call x1, Pallas kernels: 21.9 us -> 21.3 us  [dense_path(): pl.pallas_call(functools.partial(sinkhorn_kernel, n_src, n_tgt, 4), out_s...]
where the time goes in v5:
time: 23.2 us; the launch traced here: 23 us
  Pallas kernels  21.3 us (92%)
  local copies, waits for them, and re-layouts  1.11 us (5%)
  between operations  0.64 us (3%)
    pallas_call x1, Pallas kernels, dense_path(): pl.pallas_call(functools.partial(sinkhorn_kernel, n_src, n_tgt, 4), out_s...  21.3 us
    unnamed x2, local copies, waits for them, and re-layouts  1.11 us

profile of v5, /device:TPU:0, one launch (start us, length us, event | category | flops | bytes accessed | tf_op | source)
XLA Modules:
  0.0 23.0 jit_solution(17381250737587788500)
XLA Ops:
  0.6 21.3 %sinkhorn.1 = (f32[16,128]{1,0:T(8,128)S(1)}, f32[1,128]{1,0:T(1,128)S(1)}) custom-call(f32[16,64,128]{2,1,0:T(8,128)} %x_hbm.1, f32[1,64,128]{2,1,0:T(8,128)} %y_hbm.1, f32[16,128]{1,0:T(8,128)} %lms_hbm.1, f32[1,128]{1,0:T(1,128)} %lmt_hbm.1, f32[1,128]{1,0:T(1,128)} %pt_hbm.1, s32[1,8,16]{2,1,0:T(8,128)} %bitcast.2, s32[1,16]{1,0:T(1,128)} %bitcast.3), custom_call_target="tpu_custom_call" | custom-call | tf_op jit(solution)/shard_map/sinkhorn/pallas_call | solution.py:440
  21.9 0.6 %copy.11 = f32[16,128]{1,0:T(8,128)} copy(f32[16,128]{1,0:T(8,128)S(1)} %get-tuple-element.4) | data formatting | bytes 16384
  22.5 0.5 %copy.12 = f32[1,128]{1,0:T(1,128)} copy(f32[1,128]{1,0:T(1,128)S(1)} %get-tuple-element.5) | data formatting | bytes 1024
